TPU v7x, 32 devices: a whole 2x2x4 slice. The times are simulated.
32 devices in a mesh: wide: 8 (over z, y), narrow: 4 (over x, core).
Axes of the slice: x: 2, y: 2, z: 4, core: 2. Of those that a mesh axis runs over, the one named last changes fastest.
Arguments:
- prior_lt: float32 [4096, 6144], P('narrow', 'wide'), may hold values from -2 to 2
- prior_d: float32 [4096], P('narrow'), may hold values from -4 to 4
- prior_e: float32 [4096], P('narrow'), may hold values from -4 to 4
- prior_pairs: int32 [4096], P('narrow'), may hold values from 0 to 1, as said below
- pivots: int32 [2, 256], replicated, may hold values from 0 to 6143, as said below
- a_first: float32 [256, 6144], P('narrow', 'wide'), may hold values from -6 to 6
- a_second: float32 [256, 6144], P('narrow', 'wide'), may hold values from -6 to 6
- inv_d: float32 [2, 256], P(None, 'narrow'), may hold values from -4 to 4
- inv_e: float32 [2, 256], P(None, 'narrow'), may hold values from -4 to 4
- panel_pairs: int32 [2, 256], P(None, 'narrow'), may hold values from 0 to 1, as said below
Outputs:
- l_first: float32 [256, 6144], P('narrow', 'wide')
- l_second: float32 [256, 6144], P('narrow', 'wide')
Inputs may be any that keep to these rules, and one draw needn't show every extreme that they name: `pivots`: all 512 pivot rows are distinct; at most 128 of them lie in one tile of 768 consecutive rows, and some tile holds exactly 128. `prior_pairs`: 1 only at even positions; a 1 at position k joins k and k + 1 into a 2 x 2 pivot block. `panel_pairs`: 1 only at even positions along the last dimension; a 1 at position k joins k and k + 1 into a 2 x 2 pivot block.
All inputs are finite; a program needn't handle non-finite values.
Results may differ from a plain program's by a relative error of at most 0.000098.
Values sent between devices are 32-bit elements; how exact they have to be, the bound alone decides.
A program may use at most 64 MiB of HBM per device.

v0:
```python
import jax
import jax.numpy as jnp
from jax import lax
from jax.sharding import PartitionSpec as P

P_SIZE = 256


def couple(block, diag, off, pairs):
    joined = off * pairs.astype(jnp.float32)
    zero_row = jnp.zeros_like(block[:1])
    after = jnp.concatenate([block[1:], zero_row], 0)
    before = jnp.concatenate([zero_row, block[:-1]], 0)
    lower = jnp.concatenate([jnp.zeros_like(joined[:1]), joined[:-1]], 0)
    return diag[:, None] * block + joined[:, None] * after + lower[:, None] * before


def slot_layout(targets, tile_rows, capacity):
    owner = targets // tile_rows
    count = targets.shape[0]
    order = jnp.arange(count)
    same = (owner[:, None] == owner[None, :]) & (order[:, None] > order[None, :])
    rank = jnp.sum(same.astype(jnp.int32), axis=1)
    return (owner, rank, owner * capacity + rank)


def pack_local(block, targets, owner, rank, here, tile_rows, capacity):
    hit = (owner[None, :] == here) & (rank[None, :] == jnp.arange(capacity)[:, None])
    local_index = jnp.sum(jnp.where(hit, (targets % tile_rows)[None, :], 0), axis=1)
    valid = jnp.any(hit, axis=1)
    taken = jnp.take(block, local_index, axis=1)
    return jnp.where(valid[None, :], taken, 0.0)


def shards(
    prior_lt, prior_d, prior_e, prior_pairs, pivots, a_first, a_second, inv_d, inv_e, panel_pairs
):
    k_local, tile_rows = prior_lt.shape
    blocks = a_first.shape[0]
    narrow_count = lax.axis_size("narrow")
    here = lax.axis_index("wide")
    capacity = max(4 * P_SIZE // lax.axis_size("wide"), 2)
    flat = pivots.reshape(-1)
    second = pivots[1]
    owner, rank, slot = slot_layout(flat, tile_rows, capacity)
    packed = pack_local(prior_lt, flat, owner, rank, here, tile_rows, capacity)
    gathered = lax.all_gather(packed, "wide", axis=1, tiled=True)
    chosen = jnp.take(gathered, slot, axis=1)
    coupled = couple(chosen, prior_d, prior_e, prior_pairs)
    arranged = (
        coupled.reshape(k_local, 2, narrow_count, blocks)
        .transpose(0, 2, 1, 3)
        .reshape(k_local, 2 * P_SIZE)
    )
    columns = arranged
    update = lax.psum_scatter(
        lax.dot_general(
            columns, prior_lt, (((0,), (0,)), ((), ())), precision=lax.Precision.HIGHEST
        ),
        "narrow",
        scatter_dimension=0,
        tiled=True,
    )
    w_first = a_first - update[:blocks]
    l_first = couple(w_first, inv_d[0], inv_e[0], panel_pairs[0])
    owner_two, rank_two, slot_two = slot_layout(second, tile_rows, capacity)
    packed_two = pack_local(l_first, second, owner_two, rank_two, here, tile_rows, capacity)
    gathered_two = lax.all_gather(packed_two, "wide", axis=1, tiled=True)
    crossed = jnp.take(gathered_two, slot_two, axis=1)
    columns = crossed
    correction = lax.psum_scatter(
        lax.dot_general(
            columns, w_first, (((0,), (0,)), ((), ())), precision=lax.Precision.HIGHEST
        ),
        "narrow",
        scatter_dimension=0,
        tiled=True,
    )
    w_second = a_second - update[blocks:] - correction
    l_second = couple(w_second, inv_d[1], inv_e[1], panel_pairs[1])
    return (l_first, l_second)


def solution(mesh):
    in_specs = (
        P("narrow", "wide"),
        P("narrow"),
        P("narrow"),
        P("narrow"),
        P(),
        P("narrow", "wide"),
        P("narrow", "wide"),
        P(None, "narrow"),
        P(None, "narrow"),
        P(None, "narrow"),
    )
    out_specs = (P("narrow", "wide"), P("narrow", "wide"))
    return jax.shard_map(shards, mesh=mesh, in_specs=in_specs, out_specs=out_specs, check_vma=False)
```

profile of v0, /device:TPU:0, one launch (start us, length us, event | category | flops | bytes accessed | tf_op | source)
XLA Modules:
  0.0 200.7 jit_solution(961543816702302315)
XLA Ops:
  7.2 0.0 all-gather.2.cloned.1.call-start
  7.2 0.7 broadcast_divide_fusion
  7.9 0.7 and_bitcast_fusion
  8.7 0.2 convert_reduce_fusion
  8.9 0.1 select_reduce_fusion
  9.1 0.1 fusion.2
  9.2 2.4 %copy.17 = f32[1024,768]{0,1:T(8,128)S(1)} copy(f32[1024,768]{1,0:T(8,128)} %param.10) | data formatting | bytes 6291456 | tf_op args[0]
  11.6 0.0 copy-start.7
  11.6 0.0 copy-start.8
  11.6 1.6 gather_fusion
  13.2 2.0 select_bitcast_fusion.1
  15.2 0.0 all-gather.2.cloned.1.call-update
  15.2 0.0 reduce-scatter.3.cloned.1.call-start
  15.3 0.0 copy-done.7
  15.3 0.0 copy-done.8
  15.3 0.1 pad_maximum_fusion
  15.4 75.4 %all-gather.2.cloned.1.call-done = f32[1024,1024]{0,1:T(8,128)} async-done(((f32[1024,128]{0,1:T(8,128)}), f32[1024,1024]{0,1:T(8,128)}) %all-gather.2.cloned.1.call-update) | async-done | bytes 4194320 | tf_op jit(solution)/shard_map/all_gather | solution.py:47
  90.9 5.0 %gather_fusion.1 = f32[512,1024]{1,0:T(8,128)S(1)} fusion(f32[1024,1024]{0,1:T(8,128)} %all-gather.2.cloned.1.call-done, s32[1024]{0:T(1024)S(1)} %pad_clamp_fusion.2), kind=kCustom, calls=%fused_computation.1 | custom fusion | bytes 4196352 | tf_op jit(solution)/shard_map/jit(_take)/gather | solution.py:48
  95.9 0.2 select_bitcast_fusion
  96.1 0.0 copy-start.6
  96.1 0.8 fusion.18
  96.9 0.0 copy-done.6
  97.0 0.8 multiply_add_fusion
  97.8 0.0 copy-start
  97.8 0.1 copy.18
  97.9 1.7 copy-done
  99.7 0.0 copy-start.5
  99.7 0.0 copy-start.9
  99.7 0.0 copy-start.10
  99.7 0.0 copy-start.11
  99.7 0.0 copy-start.3
  99.7 6.4 %fusion.21 = f32[512,768]{1,0:T(8,128)} fusion(f32[1024,512]{0,1:T(8,128)S(1)} %bitcast.68, f32[1024,768]{1,0:T(8,128)S(1)} %copy-done), kind=kOutput, calls=%fused_computation.83 | convolution fusion | flops 4831838208 | bytes 6815744 | tf_op jit(solution)/shard_map/dot_general | solution.py:57
  106.1 0.0 reduce-scatter.3.cloned.1.call-update
  106.1 0.0 reduce-scatter.5.cloned.1.call-start
  106.2 0.0 copy-done.5
  106.3 0.0 copy-done.9
  106.3 0.0 copy-done.10
  106.3 0.1 pad_maximum_fusion.2
  106.4 0.2 convert_reduce_fusion.1
  106.6 0.1 select_reduce_fusion.1
  106.8 0.1 fusion.8
  106.9 0.0 copy-done.11
  106.9 25.9 %reduce-scatter.3.cloned.1.call-done = f32[128,768]{1,0:T(8,128)} async-done(((f32[512,768]{1,0:T(8,128)}), f32[128,768]{1,0:T(8,128)}) %reduce-scatter.3.cloned.1.call-update) | async-done | bytes 393232 | tf_op jit(solution)/shard_map/reduce_scatter | solution.py:56
  132.9 0.0 copy-done.3
  132.9 0.9 slice_subtract_fusion.1
  133.9 0.1 multiply_add_fusion.2
  134.0 0.0 copy-start.1
  134.0 0.0 copy-start.2
  134.0 0.0 copy-start.4
  134.0 0.2 copy.19
  134.2 0.6 gather_fusion.2
  134.8 0.1 select_bitcast_fusion.2
  134.9 31.5 %all_gather.7 = f32[64,1024]{0,1:T(8,128)S(1)} all-gather(f32[64,128]{0,1:T(8,128)S(1)} %select_bitcast_fusion.2), channel_id=1, replica_groups=mesh['wide'=8,'narrow'=4] {'wide'}, dimensions={1}, use_global_device_ids=true | all-gather | bytes 294912 | tf_op jit(solution)/shard_map/all_gather | solution.py:68
  166.4 0.7 gather_fusion.3
  167.2 1.7 fusion.5
  168.9 0.0 reduce-scatter.5.cloned.1.call-update
  168.9 0.1 pad_maximum_fusion.1
  169.0 23.3 %reduce-scatter.5.cloned.1.call-done = f32[64,768]{1,0:T(8,128)} async-done(((f32[256,768]{1,0:T(8,128)}), f32[64,768]{1,0:T(8,128)}) %reduce-scatter.5.cloned.1.call-update) | async-done | bytes 196624 | tf_op jit(solution)/shard_map/reduce_scatter | solution.py:71
  192.3 0.0 copy-done.2
  192.3 0.0 copy-done.4
  192.3 1.0 fusion.4
  193.3 0.0 copy-done.1
  193.3 0.8 multiply_add_fusion.1
  (30 shorter events, 0.3 us)
Async XLA Ops:
  7.2 83.7 %all-gather.2.cloned.1.call-start = ((), (), s32[]{:S(2)}) async-start(), calls=%async_computation.2 | async-start | bytes 4718592 | tf_op jit(solution)/shard_map/all_gather | solution.py:47
  11.6 3.7 %copy-start.7 = (f32[1024]{0:T(1024)S(1)}, f32[1024]{0:T(1024)}, u32[]{:S(2)}) copy-start(f32[1024]{0:T(1024)} %param.12) | copy-start | bytes 12292
  11.6 3.7 %copy-start.8 = (s32[1024]{0:T(1024)S(1)}, s32[1024]{0:T(1024)}, u32[]{:S(2)}) copy-start(s32[1024]{0:T(1024)} %param.13) | copy-start | bytes 12292
  15.2 117.7 %reduce-scatter.3.cloned.1.call-start = ((), (), s32[]{:S(2)}) async-start(), calls=%async_computation.3 | async-start | bytes 1966080 | tf_op jit(solution)/shard_map/reduce_scatter | solution.py:56
  96.1 0.9 copy-start.6
  97.8 1.9 copy-start
  99.7 6.5 %copy-start.5 = (s32[2,256]{1,0:T(2,128)S(1)}, s32[2,256]{1,0:T(2,128)}, u32[]{:S(2)}) copy-start(s32[2,256]{1,0:T(2,128)} %param.14) | copy-start | bytes 6148
  99.7 6.6 %copy-start.9 = (s32[2,64]{1,0:T(2,128)S(1)}, s32[2,64]{1,0:T(2,128)}, u32[]{:S(2)}) copy-start(s32[2,64]{1,0:T(2,128)} %param.19) | copy-start | bytes 1540
  99.7 6.6 %copy-start.10 = (f32[2,64]{1,0:T(2,128)S(1)}, f32[2,64]{1,0:T(2,128)}, u32[]{:S(2)}) copy-start(f32[2,64]{1,0:T(2,128)} %param.18) | copy-start | bytes 1540
  99.7 7.2 %copy-start.11 = (f32[2,64]{1,0:T(2,128)S(1)}, f32[2,64]{1,0:T(2,128)}, u32[]{:S(2)}) copy-start(f32[2,64]{1,0:T(2,128)} %param.17) | copy-start | bytes 1540
  99.7 33.2 %copy-start.3 = (f32[64,768]{1,0:T(8,128)S(1)}, f32[64,768]{1,0:T(8,128)}, u32[]{:S(2)}) copy-start(f32[64,768]{1,0:T(8,128)} %param.15) | copy-start | bytes 589828
  106.1 86.2 %reduce-scatter.5.cloned.1.call-start = ((), (), s32[]{:S(2)}) async-start(), calls=%async_computation.4 | async-start | bytes 983040 | tf_op jit(solution)/shard_map/reduce_scatter | solution.py:71
  134.0 59.3 %copy-start.1 = (f32[64,768]{1,0:T(8,128)}, f32[64,768]{1,0:T(8,128)S(1)}, u32[]{:S(2)}) copy-start(f32[64,768]{1,0:T(8,128)S(1)} %multiply_add_fusion.2) | copy-start | bytes 589828
  134.0 58.3 %copy-start.2 = (f32[128,768]{1,0:T(8,128)S(1)}, f32[128,768]{1,0:T(8,128)}, u32[]{:S(2)}) copy-start(f32[128,768]{1,0:T(8,128)} %reduce-scatter.3.cloned.1.call-done) | copy-start | bytes 1179652
  134.0 58.3 %copy-start.4 = (f32[64,768]{1,0:T(8,128)S(1)}, f32[64,768]{1,0:T(8,128)}, u32[]{:S(2)}) copy-start(f32[64,768]{1,0:T(8,128)} %param.16) | copy-start | bytes 589828
Sparse Core Ops, SparseCore 0:
  15.3 75.5 all-gather.1
  106.3 26.5 reduce-scatter.2
  169.0 23.2 reduce-scatter.4
where the time goes:
time: 201 us
  waiting for transfers between devices  125 us (62%)
  blocking collectives  31.5 us (16%)
  between operations  14.1 us (7%)
  local copies, waits for them, and re-layouts  13.4 us (7%)
  other arithmetic  8.62 us (4%)
  matrix products  8.14 us (4%)
    all_gather x1, waiting for transfers between devices, shards(): gathered = lax.all_gather(packed, 'wide', axis=1, tiled=True)  75.4 us
    all_gather x1, blocking collectives, shards(): gathered_two = lax.all_gather(packed_two, 'wide', axis=1, tiled=True)  31.5 us
    reduce_scatter x1, waiting for transfers between devices, shards(): lax.psum_scatter(lax.dot_general(columns, prior_lt, (((0,), (0,)), ((), (...  25.9 us
    reduce_scatter x1, waiting for transfers between devices, shards(): lax.psum_scatter(lax.dot_general(columns, w_first, (((0,), (0,)), ((), ()...  23.3 us
    dot_general x1, matrix products, shards(): lax.dot_general(columns, prior_lt, (((0,), (0,)), ((), ())), precision=la...  6.42 us
    gather x1, local copies, waits for them, and re-layouts, shards(): chosen = jnp.take(gathered, slot, axis=1)  5.01 us
    unnamed x29, local copies, waits for them, and re-layouts  4.19 us
  transfers between devices with their start and end apart: 3, of which 3 were waited for; matrix products, arithmetic and copies ran while one was open for 0% of the time, Pallas kernels for 0%

commit v1 on v0

v1 whole, which is shorter than its diff:
```python
import functools

import jax
import jax.numpy as jnp
from jax import lax
from jax.experimental import pallas as pl
from jax.experimental.pallas import tpu as pltpu
from jax.sharding import PartitionSpec as P

F32 = jnp.float32
BF16 = jnp.bfloat16
NN = (((1,), (0,)), ((), ()))
NT = (((1,), (1,)), ((), ()))


def dot(a, b, dims=NN):
    return lax.dot_general(a, b, dims, preferred_element_type=F32)


def halves(x):
    hi = x.astype(BF16)
    return hi, (x - hi.astype(F32)).astype(BF16)


def dot3(ahi, alo, bhi, blo, dims=NN):
    return dot(ahi, bhi, dims) + (dot(ahi, blo, dims) + dot(alo, bhi, dims))


def couple(block, diag, after, before, axis):
    size = block.shape[axis]
    return (
        diag * block
        + after * pltpu.roll(block, size - 1, axis)
        + before * pltpu.roll(block, 1, axis)
    )


def kernel(
    n_wide, n_narrow, cap,
    prior, kcol, krow, loc, loc_a, slot, slot_a, a_one, a_two, inv,
    l_one, l_two,
    got, got_a, dhi, dlo, chi, clo, ehi, elo, part, part2, from_core, from_core2, mid, mid2,
    from_x, from_x2, wall, turned,
    s_right, s_left, s_pair, recv, sa_right, sa_left, sa_pair, recv_a,
    s1, r1, s2, r2, s3, r3, s4, r4, s5, r5, s6, r6,
):
    k_local, tile = prior.shape
    blocks = a_one.shape[0]
    panel = blocks * n_narrow
    line = n_wide // 2
    chips = n_narrow // 2
    w = lax.axis_index("wide")
    n = lax.axis_index("narrow")
    a, b = w // 2, w % 2
    x, core = n // 2, n % 2
    pair = a * 2 + (1 - b)
    has_left, has_right = a > 0, a < line - 1

    barrier = pltpu.get_barrier_semaphore()

    def greet(**where):
        pl.semaphore_signal(barrier, inc=1, device_id=where, device_id_type=pl.DeviceIdType.MESH)

    def nar(cx, cc):
        return {"wide": w, "narrow": cx * 2 + cc}

    greet(wide=pair, narrow=n)

    @pl.when(has_left)
    def _():
        greet(wide=w - 2, narrow=n)

    @pl.when(has_right)
    def _():
        greet(wide=w + 2, narrow=n)

    greet(wide=w, narrow=x * 2 + (1 - core))
    for step in range(1, chips):
        greet(wide=w, narrow=lax.rem(x + step, chips) * 2 + core)

    pick = (loc[...] == lax.broadcasted_iota(jnp.int32, (cap, tile), 1)).astype(F32).astype(BF16)
    piece = 256
    for k in range(0, k_local, piece):
        hi, lo = halves(prior[k:k + piece, :])
        got[w, :, k:k + piece] = dot(pick, hi, NT) + dot(pick, lo, NT)
    wide_a = got_a.shape[2]
    pick_a = (loc_a[...] == lax.broadcasted_iota(jnp.int32, (wide_a, tile), 1)).astype(F32).astype(BF16)
    hi, lo = halves(a_one[...])
    got_a[w] = dot(hi, pick_a, NT) + dot(lo, pick_a, NT)

    ends = (a == 0).astype(jnp.int32) + (a == line - 1).astype(jnp.int32)
    pl.semaphore_wait(barrier, chips + 3 - ends)

    def move(buf, item, send, sem_at, rsem, to):
        return pltpu.make_async_remote_copy(
            src_ref=buf.at[item], dst_ref=buf.at[item], send_sem=send.at[sem_at], recv_sem=rsem.at[item],
            device_id={"wide": to, "narrow": n}, device_id_type=pl.DeviceIdType.MESH,
        )

    def both(item, which, to):
        at = item // 2
        return (
            move(got, item, (s_right, s_left, s_pair)[which], at, recv, to),
            move(got_a, item, (sa_right, sa_left, sa_pair)[which], at, recv_a, to),
        )

    def go(item, which, to):
        for c in both(item, which, to):
            c.start()

    def landed(item):
        for c in both(item, 0, pair):
            c.wait_recv()

    @pl.when(has_right)
    def _():
        go(w, 0, w + 2)

    @pl.when(has_left)
    def _():
        go(w, 1, w - 2)

    go(w, 2, pair)

    for k in range(0, k_local, 128):
        sl = slice(k, k + 128)
        m = couple(prior[sl, :], kcol[sl, 0:1], kcol[sl, 1:2], kcol[sl, 2:3], 0)
        hi, lo = halves(m)
        dhi[sl, :] = hi
        dlo[sl, :] = lo

    def relay(t, _):
        @pl.when(a - t >= 0)
        def _():
            item = w - 2 * t
            landed(item)
            go(item, 2, pair)

            @pl.when(has_right)
            def _():
                go(item, 0, w + 2)

        @pl.when(a + t < line)
        def _():
            item = w + 2 * t
            landed(item)
            go(item, 2, pair)

            @pl.when(has_left)
            def _():
                go(item, 1, w - 2)

        return 0

    lax.fori_loop(1, line, relay, 0)

    def from_pair(t, _):
        landed(t * 2 + (1 - b))
        return 0

    lax.fori_loop(0, line, from_pair, 0)

    slots = n_wide * cap
    put = (slot[...] == lax.broadcasted_iota(jnp.int32, (2 * panel, slots), 1)).astype(F32).astype(BF16)
    for k in range(0, k_local, piece):
        sl = slice(k, k + piece)
        hi, lo = halves(got[:, :, sl].reshape(slots, piece))
        ch, cl = dot(put, hi), dot(put, lo)
        chi[:, sl] = ch.astype(BF16)
        clo[:, sl] = cl.astype(BF16)
        c2 = ch[panel:] + cl[panel:]
        eh, el = halves(couple(c2, krow[0:1, sl], krow[1:2, sl], krow[2:3, sl], 1))
        ehi[:, sl] = eh
        elo[:, sl] = el

    def fold(v):
        return v.reshape(n_narrow, blocks, v.shape[-1])

    part[:, :, tile:] = fold(dot3(chi[:panel, :], clo[:panel, :], ehi[...], elo[...], NT))
    for c in range(0, tile, 256):
        cs = slice(c, c + 256)
        part[:, :, cs] = fold(dot3(chi[:panel, :], clo[:panel, :], dhi[:, cs], dlo[:, cs]))

    def rc(src, dst, ss, rs, to):
        return pltpu.make_async_remote_copy(
            src_ref=src, dst_ref=dst, send_sem=ss, recv_sem=rs, device_id=to, device_id_type=pl.DeviceIdType.MESH,
        )

    def chip_at(s):
        return lax.rem(x + 1 + s, chips)

    def core_swap(src, dst, ss, rs):
        return [
            rc(src.at[chip_at(s) * 2 + (1 - core)], dst.at[s], ss.at[s], rs.at[s], nar(x, 1 - core))
            for s in range(chips)
        ]

    swap1 = core_swap(part, from_core, s1, r1)
    for c in swap1:
        c.start()
    for c in range(0, tile, 256):
        cs = slice(c, c + 256)
        part2[:, :, cs] = fold(dot3(chi[panel:, :], clo[panel:, :], dhi[:, cs], dlo[:, cs]))
    swap2 = core_swap(part2, from_core2, s2, r2)
    for c in swap2:
        c.start()

    def across(swap, src, held, middle, dst, ss, rs):
        out = []
        for s in range(chips - 1):
            swap[s].wait_recv()
            middle[s] = src[chip_at(s) * 2 + core] + held[s]
            c = rc(middle.at[s], dst.at[s], ss.at[s], rs.at[s], nar(chip_at(s), core))
            c.start()
            out.append(c)
        swap[chips - 1].wait_recv()
        return out

    def total(sent, src, held, dst):
        v = src[n] + held[chips - 1]
        for s, c in enumerate(sent):
            c.wait_recv()
            v = v + dst[s]
        return v

    sent1 = across(swap1, part, from_core, mid, from_x, s3, r3)

    def gather_a(i, acc):
        hi, lo = halves(got_a[i])
        p = (slot_a[...] - i * wide_a == lax.broadcasted_iota(jnp.int32, (wide_a, panel), 0)).astype(F32).astype(BF16)
        return acc + (dot(hi, p) + dot(lo, p))

    aq = lax.fori_loop(0, n_wide, gather_a, jnp.zeros((blocks, panel), F32))
    sent2 = across(swap2, part2, from_core2, mid2, from_x2, s4, r4)

    upd = total(sent1, part, from_core, from_x)
    w_one = a_one[...] - upd[:, :tile]
    wall[n, :, :tile] = w_one
    crossed = couple(aq - upd[:, tile:], inv[:, 0:1], inv[:, 1:2], inv[:, 2:3], 0)
    wall[n, :, tile:] = crossed

    spread = [rc(wall.at[n], wall.at[n], s5.at[s], r5.at[n], nar(chip_at(s), core)) for s in range(chips - 1)]
    for c in spread:
        c.start()
    twin = [rc(wall.at[n], wall.at[n], s6.at[0], r6.at[n], nar(x, 1 - core))]
    twin[0].start()
    l_one[...] = couple(w_one, inv[:, 0:1], inv[:, 1:2], inv[:, 2:3], 0)
    w_two = a_two[...] - total(sent2, part2, from_core2, from_x2)

    for s in range(chips - 1):
        item = chip_at(s) * 2 + core
        rc(wall.at[item], wall.at[item], s5.at[s], r5.at[item], nar(x, 1 - core)).wait_recv()
        c = rc(wall.at[item], wall.at[item], s6.at[s + 1], r6.at[item], nar(x, 1 - core))
        c.start()
        twin.append(c)
    for s in range(chips):
        item = chip_at(s) * 2 + (1 - core)
        rc(wall.at[item], wall.at[item], s6.at[s], r6.at[item], nar(x, 1 - core)).wait_recv()

    turned[...] = jnp.transpose(wall[:, :, tile:].reshape(panel, panel))
    ph, plo = halves(turned[pl.ds(pl.multiple_of(n * blocks, blocks), blocks), :])
    wh, wl = halves(wall[:, :, :tile].reshape(panel, tile))
    w_two = w_two - dot3(ph, plo, wh, wl)
    l_two[...] = couple(w_two, inv[:, 3:4], inv[:, 4:5], inv[:, 5:6], 0)

    for c in swap1 + swap2 + sent1 + sent2 + spread + twin:
        c.wait_send()

    def drain(t, _):
        item = t * 2 + b
        for c in both(item, 2, pair):
            c.wait_send()

        @pl.when((t <= a) & has_right)
        def _():
            for c in both(item, 0, pair):
                c.wait_send()

        @pl.when((t >= a) & has_left)
        def _():
            for c in both(item, 1, pair):
                c.wait_send()

        return 0

    lax.fori_loop(0, line, drain, 0)


def coefficients(diag, off, pairs, axis):
    joined = off * pairs.astype(F32)
    lower = jnp.concatenate([jnp.zeros_like(joined[:1]), joined[:-1]], 0)
    return [diag, joined, lower]


def shards(
    n_wide, n_narrow,
    prior_lt, prior_d, prior_e, prior_pairs, pivots, a_first, a_second, inv_d, inv_e, panel_pairs,
):
    k_local, tile = prior_lt.shape
    blocks = a_first.shape[0]
    panel = blocks * n_narrow
    cap = max(4 * panel // n_wide, 2)
    wide_a = -(-cap // 128) * 128
    line, chips = n_wide // 2, n_narrow // 2
    here = lax.axis_index("wide")
    flat = pivots.reshape(-1)
    owner = flat // tile
    order = jnp.arange(2 * panel)
    same = (owner[:, None] == owner[None, :]) & (order[:, None] > order[None, :])
    rank = jnp.sum(same.astype(jnp.int32), axis=1)
    hit = (owner[None, :] == here) & (rank[None, :] == jnp.arange(wide_a)[:, None])
    loc = jnp.sum(jnp.where(hit, (flat - here * tile + 1)[None, :], 0), axis=1) - 1
    slot = owner * cap + rank
    slot_a = (owner * wide_a + rank)[panel:]
    parts = coefficients(prior_d, prior_e, prior_pairs, 0)
    kcol, krow = jnp.stack(parts, 1), jnp.stack(parts, 0)
    inv = jnp.stack(
        coefficients(inv_d[0], inv_e[0], panel_pairs[0], 0) + coefficients(inv_d[1], inv_e[1], panel_pairs[1], 0), 1
    )
    dma = pltpu.SemaphoreType.DMA
    vm = pltpu.VMEM
    ext = tile + panel
    out = jax.ShapeDtypeStruct((blocks, tile), F32)
    return pl.pallas_call(
        functools.partial(kernel, n_wide, n_narrow, cap),
        out_shape=(out, out),
        in_specs=[pl.BlockSpec(memory_space=vm)] * 10,
        out_specs=(pl.BlockSpec(memory_space=vm),) * 2,
        scratch_shapes=[
            vm((n_wide, cap, k_local), F32),
            vm((n_wide, blocks, wide_a), F32),
            vm((k_local, tile), BF16),
            vm((k_local, tile), BF16),
            vm((2 * panel, k_local), BF16),
            vm((2 * panel, k_local), BF16),
            vm((panel, k_local), BF16),
            vm((panel, k_local), BF16),
            vm((n_narrow, blocks, ext), F32),
            vm((n_narrow, blocks, tile), F32),
            vm((chips, blocks, ext), F32),
            vm((chips, blocks, tile), F32),
            vm((chips, blocks, ext), F32),
            vm((chips, blocks, tile), F32),
            vm((chips, blocks, ext), F32),
            vm((chips, blocks, tile), F32),
            vm((n_narrow, blocks, ext), F32),
            vm((panel, panel), F32),
            dma((line,)), dma((line,)), dma((line,)), dma((n_wide,)),
            dma((line,)), dma((line,)), dma((line,)), dma((n_wide,)),
            dma((chips,)), dma((chips,)), dma((chips,)), dma((chips,)),
            dma((chips,)), dma((chips,)), dma((chips,)), dma((chips,)),
            dma((chips,)), dma((n_narrow,)), dma((chips,)), dma((n_narrow,)),
        ],
        compiler_params=pltpu.CompilerParams(
            collective_id=0, has_side_effects=True, vmem_limit_bytes=60 * 1024 * 1024
        ),
    )(
        prior_lt, kcol, krow, loc[:cap, None], loc[:, None], slot[:, None], slot_a[None, :],
        a_first, a_second, inv,
    )


def solution(mesh):
    in_specs = (
        P("narrow", "wide"),
        P("narrow"),
        P("narrow"),
        P("narrow"),
        P(),
        P("narrow", "wide"),
        P("narrow", "wide"),
        P(None, "narrow"),
        P(None, "narrow"),
        P(None, "narrow"),
    )
    out_specs = (P("narrow", "wide"), P("narrow", "wide"))
    body = functools.partial(shards, mesh.shape["wide"], mesh.shape["narrow"])
    return jax.shard_map(body, mesh=mesh, in_specs=in_specs, out_specs=out_specs, check_vma=False)
```

time: 201 us -> 101 us (0.50)
  waiting for transfers between devices: 125 us -> 0 us
  Pallas kernels: 0 us -> 84.6 us
  blocking collectives: 31.5 us -> 0 us
  between operations: 14.1 us -> 0.7 us
  matrix products: 8.14 us -> 0 us
  local copies, waits for them, and re-layouts: 13.4 us -> 7.55 us
    pallas_call x0 -> x1, Pallas kernels: none -> 84.6 us  [shards(): pl.pallas_call(functools.partial(kernel, n_wide, n_narrow, cap), out_shap...]
    all_gather x1 -> x0, waiting for transfers between devices: 75.4 us -> none  [shards(): gathered = lax.all_gather(packed, 'wide', axis=1, tiled=True)]
    reduce_scatter x2 -> x0, waiting for transfers between devices: 49.3 us -> none  [the longest x1 25.9 us: shards(): lax.psum_scatter(lax.dot_general(columns, prior_lt, (((0,), (0,)), ((), (...]
    all_gather x1 -> x0, blocking collectives: 31.5 us -> none  [shards(): gathered_two = lax.all_gather(packed_two, 'wide', axis=1, tiled=True)]
    dot_general x2 -> x0, matrix products: 8.14 us -> none  [the longest x1 6.42 us: shards(): lax.dot_general(columns, prior_lt, (((0,), (0,)), ((), ())), precision=la...]
    gather x4 -> x0, local copies, waits for them, and re-layouts: 7.96 us -> none  [the longest x1 5.01 us: shards(): chosen = jnp.take(gathered, slot, axis=1)]
    another operation x0 -> x4, local copies, waits for them, and re-layouts: none -> 2.5 us  [the longest x3 1.49 us: shards(): jnp.stack(coefficients(inv_d[0], inv_e[0], panel_pairs[0], 0) + coefficie...]
    select_n x10 -> x0, other arithmetic: 2.33 us -> none  [the longest x2 2.06 us: pack_local(): return jnp.where(valid[None, :], taken, 0.0)]
  transfers between devices with their start and end apart: 3 -> 0, of which waited for: 3 -> 0; matrix products, arithmetic and copies ran while one was open for 0% -> 0% of each run, Pallas kernels for 0% -> 0%
where the time goes in v1:
time: 101 us; the launch traced here: 99.8 us
  Pallas kernels  84.6 us (84%)
  local copies, waits for them, and re-layouts  7.55 us (7%)
  other arithmetic  6.88 us (7%)
    pallas_call x1, Pallas kernels, shards(): pl.pallas_call(functools.partial(kernel, n_wide, n_narrow, cap), out_shap...  84.6 us
    unnamed x8, local copies, waits for them, and re-layouts  3.58 us

profile of v1, /device:TPU:0, one launch (start us, length us, event | category | flops | bytes accessed | tf_op | source)
XLA Modules:
  0.0 99.8 jit_solution(10982111987831209287)
XLA Ops:
  0.6 0.7 fusion.6
  1.3 0.7 compare_and_fusion
  2.1 0.8 slice_bitcast_fusion.1
  2.8 0.8 convert_multiply_fusion.1
  3.6 0.1 fusion.4
  3.7 0.7 broadcast_divide_fusion
  4.4 0.2 convert_reduce_fusion
  4.7 0.1 select_reduce_fusion
  4.8 0.5 slice.37
  5.4 0.7 convert_multiply_fusion
  6.1 0.1 pad_maximum_fusion.2
  6.2 0.7 pad_maximum_fusion
  6.9 1.3 %pad_maximum_fusion.1.krow = f32[3,1024]{1,0:T(4,128)} fusion(f32[1,1024]{1,0:T(1,128)S(1)} %bitcast.45, f32[1,1024]{1,0:T(1,128)S(1)} %bitcast.43, f32[1,1024]{1,0:T(1,128)} %bitcast.50), kind=kLoop, calls=%fused_computation.10 | loop fusion | flops 6144 | bytes 24576 | tf_op jit(solution)/shard_map/stack | solution.py:316
  8.2 0.7 copy.59.inv
  8.9 0.2 copy.63
  9.1 0.7 copy.57.loc.loc_a
  9.8 0.1 copy.65
  10.0 0.1 copy.55
  10.1 0.8 fusion.2.slot
  10.9 1.0 %copy.56.kcol = f32[1024,3]{1,0:T(8,128)} copy(f32[1024,3]{0,1:T(4,128)S(1)} %pad_maximum_fusion) | data formatting | bytes 24576 | tf_op jit(solution)/shard_map/stack | solution.py:316
  11.9 84.6 %shard_map.113 = (f32[64,768]{1,0:T(8,128)}, f32[64,768]{1,0:T(8,128)}) custom-call(f32[1024,768]{1,0:T(8,128)} %prior.1, f32[1024,3]{1,0:T(8,128)} %copy.56.kcol, f32[3,1024]{1,0:T(4,128)} %pad_maximum_fusion.1.krow, s32[128,1]{1,0:T(8,128)} %copy.57.loc.loc_a, s32[128,1]{1,0:T(8,128)} %copy.57.loc.loc_a, s32[512,1]{1,0:T(8,128)} %fusion.2.slot, ...), custom_call_target="tpu_custom_call" | custom-call | tf_op jit(solution)/shard_map/pallas_call | solution.py:324
  96.5 1.6 %copy.68 = f32[64,768]{1,0:T(8,128)} copy(f32[64,768]{1,0:T(8,128)} %get-tuple-element.14) | data formatting | bytes 393216
  98.1 1.6 %copy.69 = f32[64,768]{1,0:T(8,128)} copy(f32[64,768]{1,0:T(8,128)} %get-tuple-element.15) | data formatting | bytes 393216
  (11 shorter events, 0.1 us)

commit v2 on v1

v2 whole, which is shorter than its diff:
```python
import functools

import jax
import jax.numpy as jnp
from jax import lax
from jax.experimental import pallas as pl
from jax.experimental.pallas import tpu as pltpu
from jax.sharding import PartitionSpec as P

F32 = jnp.float32
BF16 = jnp.bfloat16
NN = (((1,), (0,)), ((), ()))
NT = (((1,), (1,)), ((), ()))


def dot(a, b, dims=NN):
    return lax.dot_general(a, b, dims, preferred_element_type=F32)


def halves(x):
    hi = x.astype(BF16)
    return hi, (x - hi.astype(F32)).astype(BF16)


def dot3(ahi, alo, bhi, blo, dims=NN):
    return dot(ahi, bhi, dims) + (dot(ahi, blo, dims) + dot(alo, bhi, dims))


def couple(block, diag, joined, axis):
    size = block.shape[axis]
    return diag * block + joined * pltpu.roll(block, size - 1, axis) + pltpu.roll(joined * block, 1, axis)


def count(shape, axis):
    return lax.broadcasted_iota(jnp.int32, shape, axis).astype(F32)


def column(row):
    size = row.shape[1]
    step = min(size, 128)
    eye = count((step, step), 0) == count((step, step), 1)
    return jnp.concatenate(
        [jnp.sum(jnp.where(eye, row[:, i:i + step], 0.0), axis=1, keepdims=True) for i in range(0, size, step)], 0
    )


def onehot(mask):
    return jnp.where(mask, 1.0, 0.0).astype(BF16)


def kernel(
    n_wide, n_narrow, cap, pieces,
    prior_hbm, diag, off, pairs, pivots, a_one, a_two, inv_d, inv_e, panel_pairs,
    l_one, l_two,
    prior, packed, inbox, dense, got_a, put, coef, dhi, dlo, part, part2, from_core, from_core2, mid, mid2,
    from_x, from_x2, wall, turned,
    s_load, s_post, r_post,
    s_right, s_left, s_pair, recv, sa_right, sa_left, sa_pair, recv_a,
    s1, r1, s2, r2, s3, r3, s4, r4, s5, r5, s6, r6,
):
    k_local, tile = prior.shape
    blocks = a_one.shape[0]
    panel = blocks * n_narrow
    kk = k_local // pieces
    line = n_wide // 2
    held = pieces // 2
    chips = n_narrow // 2
    wide_a = got_a.shape[2]
    w = lax.axis_index("wide")
    n = lax.axis_index("narrow")
    a, b = w // 2, w % 2
    x, core = n // 2, n % 2
    pair = a * 2 + (1 - b)
    has_left, has_right = a > 0, a < line - 1
    mesh_ids = pl.DeviceIdType.MESH

    loads = [
        pltpu.make_async_copy(prior_hbm.at[pl.ds(q * kk, kk)], prior.at[pl.ds(q * kk, kk)], s_load.at[q])
        for q in range(pieces)
    ]
    for c in loads:
        c.start()

    barrier = pltpu.get_barrier_semaphore()

    def greet(to, which):
        pl.semaphore_signal(barrier, inc=1, device_id={"wide": to, "narrow": which}, device_id_type=mesh_ids)

    def greet_wide(i, _):
        greet(lax.rem(w + i, n_wide), n)
        return 0

    lax.fori_loop(1, n_wide, greet_wide, 0)

    def nar(cx, cc):
        return {"wide": w, "narrow": cx * 2 + cc}

    greet(w, x * 2 + (1 - core))
    for step in range(1, chips):
        greet(w, lax.rem(x + step, chips) * 2 + core)

    flat = jnp.concatenate([pivots[0:1, :], pivots[1:2, :]], 1).astype(F32)
    owner = jnp.floor((flat + 0.5) * (1.0 / tile))
    square = (2 * panel, 2 * panel)
    same = (column(owner) == owner) & (count(square, 0) < count(square, 1))
    rank = jnp.sum(jnp.where(same, 1.0, 0.0), axis=0, keepdims=True)
    here = w.astype(F32)
    hit = (owner == here) & (rank == count((wide_a, 2 * panel), 0))
    loc = jnp.sum(jnp.where(hit, flat - here * tile + 1.0, 0.0), axis=1, keepdims=True) - 1.0
    pick_a = onehot(loc == count((wide_a, tile), 1))
    pick = pick_a[:cap]

    pl.semaphore_wait(barrier, n_wide - 1 + chips)

    def post(q):
        return pltpu.make_async_remote_copy(
            src_ref=packed.at[q], dst_ref=inbox.at[w], send_sem=s_post.at[q], recv_sem=r_post.at[w],
            device_id={"wide": q, "narrow": n}, device_id_type=mesh_ids,
        )

    for q in range(pieces):
        loads[q].wait()
        hi, lo = halves(prior[q * kk:(q + 1) * kk, :])
        packed[q] = dot(pick, hi, NT) + dot(pick, lo, NT)

        @pl.when(w != q)
        def _():
            post(q).start()

    def move(buf, item, send, sem_at, rsem, to):
        return pltpu.make_async_remote_copy(
            src_ref=buf.at[item], dst_ref=buf.at[item], send_sem=send.at[sem_at], recv_sem=rsem.at[item],
            device_id={"wide": to, "narrow": n}, device_id_type=mesh_ids,
        )

    def piece_to(item, which, to):
        return move(dense, item, (s_right, s_left, s_pair)[which], item // 2, recv, to)

    def a_to(item, which, to):
        return move(got_a, item, (sa_right, sa_left, sa_pair)[which], item // 2, recv_a, to)

    def send_own(make):
        @pl.when(has_right)
        def _():
            make(w, 0, w + 2).start()

        @pl.when(has_left)
        def _():
            make(w, 1, w - 2).start()

        make(w, 2, pair).start()

    hi, lo = halves(a_one[...])
    got_a[w] = dot(hi, pick_a, NT) + dot(lo, pick_a, NT)
    send_own(a_to)

    slots = n_wide * cap
    put[...] = onehot(column(owner * cap + rank) == count((2 * panel, slots), 1))
    joined = off[...] * pairs[...].astype(F32)
    for q in range(pieces):
        sl = slice(q * kk, (q + 1) * kk)
        coef[q, 0:1, :] = diag[:, sl]
        coef[q, 1:2, :] = joined[:, sl]

    @pl.when(w < pieces)
    def _():
        inbox[w] = packed[w]

        def arrived(j, _):
            @pl.when(j != w)
            def _():
                pltpu.make_async_remote_copy(
                    src_ref=packed.at[0], dst_ref=inbox.at[j], send_sem=s_post.at[0], recv_sem=r_post.at[j],
                    device_id={"wide": pair, "narrow": n}, device_id_type=mesh_ids,
                ).wait_recv()

            return 0

        lax.fori_loop(0, n_wide, arrived, 0)
        hi, lo = halves(inbox[...].reshape(slots, kk))
        dense[w] = dot(put[...], hi) + dot(put[...], lo)
        send_own(piece_to)

    for q in range(pieces):
        sl = slice(q * kk, (q + 1) * kk)
        m = couple(prior[sl, :], column(diag[:, sl]), column(joined[:, sl]), 0)
        hi, lo = halves(m)
        dhi[sl, :] = hi
        dlo[sl, :] = lo
    part[...] = jnp.zeros_like(part)
    part2[...] = jnp.zeros_like(part2)

    inv_j = inv_e[...] * panel_pairs[...].astype(F32)
    inv = [(column(inv_d[i:i + 1, :]), column(inv_j[i:i + 1, :])) for i in range(2)]

    def fold(v):
        return v.reshape(n_narrow, blocks, v.shape[-1])

    def add_pair(p):
        c = [dense[2 * p + i] for i in range(2)]
        e = [
            halves(couple(c[i][panel:], coef[2 * p + i, 0:1, :], coef[2 * p + i, 1:2, :], 1)) for i in range(2)
        ]
        c = [halves(v) for v in c]
        ch, cl = (jnp.concatenate([c[0][i], c[1][i]], 1) for i in range(2))
        eh, el = (jnp.concatenate([e[0][i], e[1][i]], 1) for i in range(2))
        rows = pl.ds(pl.multiple_of(p * 2 * kk, 2 * kk), 2 * kk)
        part[:, :, tile:] += fold(dot3(ch[:panel], cl[:panel], eh, el, NT))
        for j in range(0, tile, 256):
            cs = slice(j, j + 256)
            ph, pq = dhi[rows, cs], dlo[rows, cs]
            part[:, :, cs] += fold(dot3(ch[:panel], cl[:panel], ph, pq))
            part2[:, :, cs] += fold(dot3(ch[panel:], cl[panel:], ph, pq))

    def relay_item(make, item, ahead, which, to):
        make(item, 0, pair).wait_recv()
        make(item, 2, pair).start()

        @pl.when(ahead)
        def _():
            make(item, which, to).start()

    def step(t, _):
        for make, size in ((a_to, line), (piece_to, held)):
            @pl.when((t < line) & (a - t >= 0) & (a - t < size))
            def _():
                relay_item(make, w - 2 * t, has_right, 0, w + 2)

            @pl.when((t < line) & (a + t < size))
            def _():
                relay_item(make, w + 2 * t, has_left, 1, w - 2)

        def pair_at(p):
            piece_to(2 * p + (1 - b), 0, pair).wait_recv()
            add_pair(p)

        @pl.when((a - t + 1 >= 0) & (a - t + 1 < held))
        def _():
            pair_at(a - t + 1)

        @pl.when((t > 1) & (a + t - 1 < held))
        def _():
            pair_at(a + t - 1)

        return 0

    lax.fori_loop(1, line + 1, step, 0)

    def rc(src, dst, ss, rs, to):
        return pltpu.make_async_remote_copy(
            src_ref=src, dst_ref=dst, send_sem=ss, recv_sem=rs, device_id=to, device_id_type=pl.DeviceIdType.MESH,
        )

    def chip_at(s):
        return lax.rem(x + 1 + s, chips)

    def core_swap(src, dst, ss, rs):
        return [
            rc(src.at[chip_at(s) * 2 + (1 - core)], dst.at[s], ss.at[s], rs.at[s], nar(x, 1 - core))
            for s in range(chips)
        ]

    swap1 = core_swap(part, from_core, s1, r1)
    for c in swap1:
        c.start()
    swap2 = core_swap(part2, from_core2, s2, r2)
    for c in swap2:
        c.start()

    def across(swap, src, partner, middle, dst, ss, rs):
        out = []
        for s in range(chips - 1):
            swap[s].wait_recv()
            middle[s] = src[chip_at(s) * 2 + core] + partner[s]
            c = rc(middle.at[s], dst.at[s], ss.at[s], rs.at[s], nar(chip_at(s), core))
            c.start()
            out.append(c)
        swap[chips - 1].wait_recv()
        return out

    def total(sent, src, partner, dst):
        v = src[n] + partner[chips - 1]
        for s, c in enumerate(sent):
            c.wait_recv()
            v = v + dst[s]
        return v

    sent1 = across(swap1, part, from_core, mid, from_x, s3, r3)

    def from_pair(t, _):
        a_to(t * 2 + (1 - b), 0, pair).wait_recv()
        return 0

    lax.fori_loop(0, line, from_pair, 0)
    slot_a = owner[:, panel:] * wide_a + rank[:, panel:]

    def gather_a(i, acc):
        hi, lo = halves(got_a[i])
        p = onehot(slot_a == count((wide_a, panel), 0) + (i * wide_a).astype(F32))
        return acc + (dot(hi, p) + dot(lo, p))

    aq = lax.fori_loop(0, n_wide, gather_a, jnp.zeros((blocks, panel), F32))
    sent2 = across(swap2, part2, from_core2, mid2, from_x2, s4, r4)

    upd = total(sent1, part, from_core, from_x)
    w_one = a_one[...] - upd[:, :tile]
    wall[n, :, :tile] = w_one
    crossed = couple(aq - upd[:, tile:], *inv[0], 0)
    wall[n, :, tile:] = crossed

    spread = [rc(wall.at[n], wall.at[n], s5.at[s], r5.at[n], nar(chip_at(s), core)) for s in range(chips - 1)]
    for c in spread:
        c.start()
    twin = [rc(wall.at[n], wall.at[n], s6.at[0], r6.at[n], nar(x, 1 - core))]
    twin[0].start()
    l_one[...] = couple(w_one, *inv[0], 0)
    w_two = a_two[...] - total(sent2, part2, from_core2, from_x2)

    for s in range(chips - 1):
        item = chip_at(s) * 2 + core
        rc(wall.at[item], wall.at[item], s5.at[s], r5.at[item], nar(x, 1 - core)).wait_recv()
        c = rc(wall.at[item], wall.at[item], s6.at[s + 1], r6.at[item], nar(x, 1 - core))
        c.start()
        twin.append(c)
    for s in range(chips):
        item = chip_at(s) * 2 + (1 - core)
        rc(wall.at[item], wall.at[item], s6.at[s], r6.at[item], nar(x, 1 - core)).wait_recv()

    turned[...] = jnp.transpose(wall[:, :, tile:].reshape(panel, panel))
    ph, plo = halves(turned[pl.ds(pl.multiple_of(n * blocks, blocks), blocks), :])
    wh, wl = halves(wall[:, :, :tile].reshape(panel, tile))
    w_two = w_two - dot3(ph, plo, wh, wl)
    l_two[...] = couple(w_two, *inv[1], 0)

    for c in swap1 + swap2 + sent1 + sent2 + spread + twin:
        c.wait_send()
    for q in range(pieces):
        @pl.when(w != q)
        def _():
            post(q).wait_send()

    def drain(t, _):
        item = t * 2 + b
        for make, size in ((a_to, line), (piece_to, held)):
            @pl.when(t < size)
            def _():
                make(item, 2, pair).wait_send()

            @pl.when((t < size) & (t <= a) & has_right)
            def _():
                make(item, 0, pair).wait_send()

            @pl.when((t < size) & (t >= a) & has_left)
            def _():
                make(item, 1, pair).wait_send()

        return 0

    lax.fori_loop(0, line, drain, 0)


def shards(
    n_wide, n_narrow,
    prior_lt, prior_d, prior_e, prior_pairs, pivots, a_first, a_second, inv_d, inv_e, panel_pairs,
):
    k_local, tile = prior_lt.shape
    blocks = a_first.shape[0]
    panel = blocks * n_narrow
    cap = max(4 * panel // n_wide, 2)
    wide_a = -(-cap // 128) * 128
    line, chips = n_wide // 2, n_narrow // 2
    pieces = min(n_wide, k_local // 128)
    kk = k_local // pieces
    dma = pltpu.SemaphoreType.DMA
    vm = pltpu.VMEM
    ext = tile + panel
    out = jax.ShapeDtypeStruct((blocks, tile), F32)
    return pl.pallas_call(
        functools.partial(kernel, n_wide, n_narrow, cap, pieces),
        out_shape=(out, out),
        in_specs=[pl.BlockSpec(memory_space=pl.ANY)] + [pl.BlockSpec(memory_space=vm)] * 9,
        out_specs=(pl.BlockSpec(memory_space=vm),) * 2,
        scratch_shapes=[
            vm((k_local, tile), F32),
            vm((pieces, cap, kk), F32),
            vm((n_wide, cap, kk), F32),
            vm((pieces, 2 * panel, kk), F32),
            vm((n_wide, blocks, wide_a), F32),
            vm((2 * panel, n_wide * cap), BF16),
            vm((pieces, 8, kk), F32),
            vm((k_local, tile), BF16),
            vm((k_local, tile), BF16),
            vm((n_narrow, blocks, ext), F32),
            vm((n_narrow, blocks, tile), F32),
            vm((chips, blocks, ext), F32),
            vm((chips, blocks, tile), F32),
            vm((chips, blocks, ext), F32),
            vm((chips, blocks, tile), F32),
            vm((chips, blocks, ext), F32),
            vm((chips, blocks, tile), F32),
            vm((n_narrow, blocks, ext), F32),
            vm((panel, panel), F32),
            dma((pieces,)), dma((pieces,)), dma((n_wide,)),
            dma((line,)), dma((line,)), dma((line,)), dma((pieces,)),
            dma((line,)), dma((line,)), dma((line,)), dma((n_wide,)),
            dma((chips,)), dma((chips,)), dma((chips,)), dma((chips,)),
            dma((chips,)), dma((chips,)), dma((chips,)), dma((chips,)),
            dma((chips,)), dma((n_narrow,)), dma((chips,)), dma((n_narrow,)),
        ],
        compiler_params=pltpu.CompilerParams(
            collective_id=0, has_side_effects=True, vmem_limit_bytes=60 * 1024 * 1024
        ),
    )(
        prior_lt, prior_d[None, :], prior_e[None, :], prior_pairs[None, :], pivots,
        a_first, a_second, inv_d, inv_e, panel_pairs,
    )


def solution(mesh):
    in_specs = (
        P("narrow", "wide"),
        P("narrow"),
        P("narrow"),
        P("narrow"),
        P(),
        P("narrow", "wide"),
        P("narrow", "wide"),
        P(None, "narrow"),
        P(None, "narrow"),
        P(None, "narrow"),
    )
    out_specs = (P("narrow", "wide"), P("narrow", "wide"))
    body = functools.partial(shards, mesh.shape["wide"], mesh.shape["narrow"])
    return jax.shard_map(body, mesh=mesh, in_specs=in_specs, out_specs=out_specs, check_vma=False)
```

time: 101 us -> 74 us (0.73); the launches traced: 99.8 us -> 73.8 us
  Pallas kernels: 84.6 us -> 69.9 us
  other arithmetic: 6.88 us -> 0 us
  local copies, waits for them, and re-layouts: 7.55 us -> 3.23 us
    pallas_call x1, Pallas kernels: 84.6 us -> 69.9 us  [shards(): pl.pallas_call(functools.partial(kernel, n_wide, n_narrow, cap, pieces),...]
    another operation x4 -> x0, local copies, waits for them, and re-layouts: 2.5 us -> none  [the longest x3 1.49 us: shards(): jnp.stack(coefficients(inv_d[0], inv_e[0], panel_pairs[0], 0) + coefficie...]
    another operation x3 -> x0, other arithmetic: 2.08 us -> none  [the longest x2 2 us: shards(): kcol, krow = (jnp.stack(parts, 1), jnp.stack(parts, 0))]
    mul x2 -> x0, other arithmetic: 1.47 us -> none  [coefficients(): joined = off * pairs.astype(F32)]
    unnamed x8 -> x2, local copies, waits for them, and re-layouts: 3.58 us -> 3.23 us
where the time goes in v2:
time: 74 us; the launch traced here: 73.8 us
  Pallas kernels  69.9 us (94%)
  local copies, waits for them, and re-layouts  3.23 us (4%)
    pallas_call x1, Pallas kernels, shards(): pl.pallas_call(functools.partial(kernel, n_wide, n_narrow, cap, pieces),...  69.9 us
    unnamed x2, local copies, waits for them, and re-layouts  3.23 us

profile of v2, /device:TPU:0, one launch (start us, length us, event | category | flops | bytes accessed | tf_op | source)
XLA Modules:
  0.0 73.8 jit_solution(9156142032579185265)
XLA Ops:
  0.6 69.9 %shard_map.113 = (f32[64,768]{1,0:T(8,128)}, f32[64,768]{1,0:T(8,128)}) custom-call(f32[1024,768]{1,0:T(8,128)} %prior_hbm.1, f32[1,1024]{1,0:T(1,128)} %bitcast.3, f32[1,1024]{1,0:T(1,128)} %bitcast.4, s32[1,1024]{1,0:T(1,128)} %bitcast.5, s32[2,256]{1,0:T(2,128)} %pivots.1, f32[64,768]{1,0:T(8,128)} %a_one.1, f32[64,768]{1,0:T(8,128)} %a_two.1, ...), custom_call_target="tpu_custom_call" | custom-call | tf_op jit(solution)/shard_map/pallas_call | solution.py:378
  70.6 1.6 %copy.14 = f32[64,768]{1,0:T(8,128)} copy(f32[64,768]{1,0:T(8,128)} %get-tuple-element.4) | data formatting | bytes 393216
  72.2 1.6 %copy.15 = f32[64,768]{1,0:T(8,128)} copy(f32[64,768]{1,0:T(8,128)} %get-tuple-element.5) | data formatting | bytes 393216

commit v3 on v2

--- a/solution.py
+++ b/solution.py
@@ -26,9 +26,12 @@
     return dot(ahi, bhi, dims) + (dot(ahi, blo, dims) + dot(alo, bhi, dims))
 
 
+def beside(block, joined, axis):
+    return joined * pltpu.roll(block, block.shape[axis] - 1, axis) + pltpu.roll(joined * block, 1, axis)
+
+
 def couple(block, diag, joined, axis):
-    size = block.shape[axis]
-    return diag * block + joined * pltpu.roll(block, size - 1, axis) + pltpu.roll(joined * block, 1, axis)
+    return diag * block + beside(block, joined, axis)
 
 
 def count(shape, axis):
@@ -51,11 +54,11 @@
 def kernel(
     n_wide, n_narrow, cap, pieces,
     prior_hbm, diag, off, pairs, pivots, a_one, a_two, inv_d, inv_e, panel_pairs,
-    l_one, l_two,
-    prior, packed, inbox, dense, got_a, put, coef, dhi, dlo, part, part2, from_core, from_core2, mid, mid2,
+    l_one, l_two, side_one, side_two,
+    prior, packed, inbox, dense, put, put_a, coef, dhi, dlo, part, part2, from_core, from_core2, mid, mid2,
     from_x, from_x2, wall, turned,
     s_load, s_post, r_post,
-    s_right, s_left, s_pair, recv, sa_right, sa_left, sa_pair, recv_a,
+    s_right, s_left, s_pair, recv,
     s1, r1, s2, r2, s3, r3, s4, r4, s5, r5, s6, r6,
 ):
     k_local, tile = prior.shape
@@ -65,7 +68,8 @@
     line = n_wide // 2
     held = pieces // 2
     chips = n_narrow // 2
-    wide_a = got_a.shape[2]
+    rows_a = blocks // pieces
+    strips = panel // kk
     w = lax.axis_index("wide")
     n = lax.axis_index("narrow")
     a, b = w // 2, w % 2
@@ -105,9 +109,9 @@
     same = (column(owner) == owner) & (count(square, 0) < count(square, 1))
     rank = jnp.sum(jnp.where(same, 1.0, 0.0), axis=0, keepdims=True)
     here = w.astype(F32)
-    hit = (owner == here) & (rank == count((wide_a, 2 * panel), 0))
+    hit = (owner == here) & (rank == count((kk, 2 * panel), 0))
     loc = jnp.sum(jnp.where(hit, flat - here * tile + 1.0, 0.0), axis=1, keepdims=True) - 1.0
-    pick_a = onehot(loc == count((wide_a, tile), 1))
+    pick_a = onehot(loc == count((kk, tile), 1))
     pick = pick_a[:cap]
 
     pl.semaphore_wait(barrier, n_wide - 1 + chips)
@@ -118,10 +122,14 @@
             device_id={"wide": q, "narrow": n}, device_id_type=mesh_ids,
         )
 
+    hi, lo = halves(a_one[...])
+    packed_a = dot(hi, pick_a, NT) + dot(lo, pick_a, NT)
+    for q in range(pieces):
+        packed[q, cap:, :] = packed_a[q * rows_a:(q + 1) * rows_a, :]
     for q in range(pieces):
         loads[q].wait()
         hi, lo = halves(prior[q * kk:(q + 1) * kk, :])
-        packed[q] = dot(pick, hi, NT) + dot(pick, lo, NT)
+        packed[q, :cap, :] = dot(pick, hi, NT) + dot(pick, lo, NT)
 
         @pl.when(w != q)
         def _():
@@ -136,9 +144,6 @@
     def piece_to(item, which, to):
         return move(dense, item, (s_right, s_left, s_pair)[which], item // 2, recv, to)
 
-    def a_to(item, which, to):
-        return move(got_a, item, (sa_right, sa_left, sa_pair)[which], item // 2, recv_a, to)
-
     def send_own(make):
         @pl.when(has_right)
         def _():
@@ -149,10 +154,6 @@
             make(w, 1, w - 2).start()
 
         make(w, 2, pair).start()
-
-    hi, lo = halves(a_one[...])
-    got_a[w] = dot(hi, pick_a, NT) + dot(lo, pick_a, NT)
-    send_own(a_to)
 
     slots = n_wide * cap
     put[...] = onehot(column(owner * cap + rank) == count((2 * panel, slots), 1))
@@ -162,24 +163,8 @@
         coef[q, 0:1, :] = diag[:, sl]
         coef[q, 1:2, :] = joined[:, sl]
 
-    @pl.when(w < pieces)
-    def _():
-        inbox[w] = packed[w]
-
-        def arrived(j, _):
-            @pl.when(j != w)
-            def _():
-                pltpu.make_async_remote_copy(
-                    src_ref=packed.at[0], dst_ref=inbox.at[j], send_sem=s_post.at[0], recv_sem=r_post.at[j],
-                    device_id={"wide": pair, "narrow": n}, device_id_type=mesh_ids,
-                ).wait_recv()
-
-            return 0
-
-        lax.fori_loop(0, n_wide, arrived, 0)
-        hi, lo = halves(inbox[...].reshape(slots, kk))
-        dense[w] = dot(put[...], hi) + dot(put[...], lo)
-        send_own(piece_to)
+    slot_a = owner[:, panel:] * kk + rank[:, panel:]
+    put_a[...] = onehot(slot_a == count((n_wide * kk, panel), 0))
 
     for q in range(pieces):
         sl = slice(q * kk, (q + 1) * kk)
@@ -193,11 +178,34 @@
     inv_j = inv_e[...] * panel_pairs[...].astype(F32)
     inv = [(column(inv_d[i:i + 1, :]), column(inv_j[i:i + 1, :])) for i in range(2)]
 
+    @pl.when(w < pieces)
+    def _():
+        inbox[w] = packed[w]
+
+        def arrived(j, _):
+            @pl.when(j != w)
+            def _():
+                pltpu.make_async_remote_copy(
+                    src_ref=packed.at[0], dst_ref=inbox.at[j], send_sem=s_post.at[0], recv_sem=r_post.at[j],
+                    device_id={"wide": pair, "narrow": n}, device_id_type=mesh_ids,
+                ).wait_recv()
+
+            return 0
+
+        lax.fori_loop(0, n_wide, arrived, 0)
+        hi, lo = halves(inbox[:, :cap, :].reshape(slots, kk))
+        dense[w, :2 * panel, :] = dot(put[...], hi) + dot(put[...], lo)
+        hi, lo = halves(jnp.concatenate([inbox[j, cap:, :] for j in range(n_wide)], 1))
+        ordered = dot(hi, put_a[...]) + dot(lo, put_a[...])
+        for i in range(strips):
+            dense[w, 2 * panel + i * rows_a:2 * panel + (i + 1) * rows_a, :] = ordered[:, i * kk:(i + 1) * kk]
+        send_own(piece_to)
+
     def fold(v):
         return v.reshape(n_narrow, blocks, v.shape[-1])
 
     def add_pair(p):
-        c = [dense[2 * p + i] for i in range(2)]
+        c = [dense[2 * p + i, :2 * panel, :] for i in range(2)]
         e = [
             halves(couple(c[i][panel:], coef[2 * p + i, 0:1, :], coef[2 * p + i, 1:2, :], 1)) for i in range(2)
         ]
@@ -221,14 +229,13 @@
             make(item, which, to).start()
 
     def step(t, _):
-        for make, size in ((a_to, line), (piece_to, held)):
-            @pl.when((t < line) & (a - t >= 0) & (a - t < size))
-            def _():
-                relay_item(make, w - 2 * t, has_right, 0, w + 2)
-
-            @pl.when((t < line) & (a + t < size))
-            def _():
-                relay_item(make, w + 2 * t, has_left, 1, w - 2)
+        @pl.when((t < line) & (a - t >= 0) & (a - t < held))
+        def _():
+            relay_item(piece_to, w - 2 * t, has_right, 0, w + 2)
+
+        @pl.when((t < line) & (a + t < held))
+        def _():
+            relay_item(piece_to, w + 2 * t, has_left, 1, w - 2)
 
         def pair_at(p):
             piece_to(2 * p + (1 - b), 0, pair).wait_recv()
@@ -287,19 +294,9 @@
 
     sent1 = across(swap1, part, from_core, mid, from_x, s3, r3)
 
-    def from_pair(t, _):
-        a_to(t * 2 + (1 - b), 0, pair).wait_recv()
-        return 0
-
-    lax.fori_loop(0, line, from_pair, 0)
-    slot_a = owner[:, panel:] * wide_a + rank[:, panel:]
-
-    def gather_a(i, acc):
-        hi, lo = halves(got_a[i])
-        p = onehot(slot_a == count((wide_a, panel), 0) + (i * wide_a).astype(F32))
-        return acc + (dot(hi, p) + dot(lo, p))
-
-    aq = lax.fori_loop(0, n_wide, gather_a, jnp.zeros((blocks, panel), F32))
+    aq = jnp.concatenate(
+        [dense[:, 2 * panel + i * rows_a:2 * panel + (i + 1) * rows_a, :].reshape(blocks, kk) for i in range(strips)], 1
+    )
     sent2 = across(swap2, part2, from_core2, mid2, from_x2, s4, r4)
 
     upd = total(sent1, part, from_core, from_x)
@@ -313,7 +310,8 @@
         c.start()
     twin = [rc(wall.at[n], wall.at[n], s6.at[0], r6.at[n], nar(x, 1 - core))]
     twin[0].start()
-    l_one[...] = couple(w_one, *inv[0], 0)
+    l_one[...] = w_one
+    side_one[...] = beside(w_one, inv[0][1], 0)
     w_two = a_two[...] - total(sent2, part2, from_core2, from_x2)
 
     for s in range(chips - 1):
@@ -330,7 +328,8 @@
     ph, plo = halves(turned[pl.ds(pl.multiple_of(n * blocks, blocks), blocks), :])
     wh, wl = halves(wall[:, :, :tile].reshape(panel, tile))
     w_two = w_two - dot3(ph, plo, wh, wl)
-    l_two[...] = couple(w_two, *inv[1], 0)
+    l_two[...] = w_two
+    side_two[...] = beside(w_two, inv[1][1], 0)
 
     for c in swap1 + swap2 + sent1 + sent2 + spread + twin:
         c.wait_send()
@@ -341,22 +340,19 @@
 
     def drain(t, _):
         item = t * 2 + b
-        for make, size in ((a_to, line), (piece_to, held)):
-            @pl.when(t < size)
-            def _():
-                make(item, 2, pair).wait_send()
-
-            @pl.when((t < size) & (t <= a) & has_right)
-            def _():
-                make(item, 0, pair).wait_send()
-
-            @pl.when((t < size) & (t >= a) & has_left)
-            def _():
-                make(item, 1, pair).wait_send()
+        piece_to(item, 2, pair).wait_send()
+
+        @pl.when((t <= a) & has_right)
+        def _():
+            piece_to(item, 0, pair).wait_send()
+
+        @pl.when((t >= a) & has_left)
+        def _():
+            piece_to(item, 1, pair).wait_send()
 
         return 0
 
-    lax.fori_loop(0, line, drain, 0)
+    lax.fori_loop(0, held, drain, 0)
 
 
 def shards(
@@ -367,26 +363,26 @@
     blocks = a_first.shape[0]
     panel = blocks * n_narrow
     cap = max(4 * panel // n_wide, 2)
-    wide_a = -(-cap // 128) * 128
     line, chips = n_wide // 2, n_narrow // 2
     pieces = min(n_wide, k_local // 128)
     kk = k_local // pieces
+    rows_a, strips = blocks // pieces, panel // kk
     dma = pltpu.SemaphoreType.DMA
     vm = pltpu.VMEM
     ext = tile + panel
     out = jax.ShapeDtypeStruct((blocks, tile), F32)
-    return pl.pallas_call(
+    w_one, w_two, side_one, side_two = pl.pallas_call(
         functools.partial(kernel, n_wide, n_narrow, cap, pieces),
-        out_shape=(out, out),
+        out_shape=(out,) * 4,
         in_specs=[pl.BlockSpec(memory_space=pl.ANY)] + [pl.BlockSpec(memory_space=vm)] * 9,
-        out_specs=(pl.BlockSpec(memory_space=vm),) * 2,
+        out_specs=(pl.BlockSpec(memory_space=vm),) * 4,
         scratch_shapes=[
             vm((k_local, tile), F32),
-            vm((pieces, cap, kk), F32),
-            vm((n_wide, cap, kk), F32),
-            vm((pieces, 2 * panel, kk), F32),
-            vm((n_wide, blocks, wide_a), F32),
+            vm((pieces, cap + rows_a, kk), F32),
+            vm((n_wide, cap + rows_a, kk), F32),
+            vm((pieces, 2 * panel + strips * rows_a, kk), F32),
             vm((2 * panel, n_wide * cap), BF16),
+            vm((n_wide * kk, panel), BF16),
             vm((pieces, 8, kk), F32),
             vm((k_local, tile), BF16),
             vm((k_local, tile), BF16),
@@ -402,7 +398,6 @@
             vm((panel, panel), F32),
             dma((pieces,)), dma((pieces,)), dma((n_wide,)),
             dma((line,)), dma((line,)), dma((line,)), dma((pieces,)),
-            dma((line,)), dma((line,)), dma((line,)), dma((n_wide,)),
             dma((chips,)), dma((chips,)), dma((chips,)), dma((chips,)),
             dma((chips,)), dma((chips,)), dma((chips,)), dma((chips,)),
             dma((chips,)), dma((n_narrow,)), dma((chips,)), dma((n_narrow,)),
@@ -414,6 +409,7 @@
         prior_lt, prior_d[None, :], prior_e[None, :], prior_pairs[None, :], pivots,
         a_first, a_second, inv_d, inv_e, panel_pairs,
     )
+    return inv_d[0][:, None] * w_one + side_one, inv_d[1][:, None] * w_two + side_two
 
 
 def solution(mesh):

time: 74 us -> 73.9 us (level)
  local copies, waits for them, and re-layouts: 3.23 us -> 0.76 us
  other arithmetic: 0 us -> 2.07 us
    unnamed x2 -> x0, local copies, waits for them, and re-layouts: 3.23 us -> none
    add x0 -> x1, other arithmetic: none -> 2.07 us  [shards(): inv_d[1][:, None] * w_two + side_two]
    mul x0 -> x1, local copies, waits for them, and re-layouts: none -> 0.76 us  [shards(): inv_d[1][:, None] * w_two + side_two]
where the time goes in v3:
time: 73.9 us; the launch traced here: 73.7 us
  Pallas kernels  70.3 us (95%)
  other arithmetic  2.07 us (3%)
  local copies, waits for them, and re-layouts  0.76 us (1%)
    pallas_call x1, Pallas kernels, shards(): pl.pallas_call(functools.partial(kernel, n_wide, n_narrow, cap, pieces),...  70.3 us
    add x1, other arithmetic, shards(): inv_d[1][:, None] * w_two + side_two  2.07 us

profile of v3, /device:TPU:0, one launch (start us, length us, event | category | flops | bytes accessed | tf_op | source)
XLA Modules:
  0.0 73.7 jit_solution(7098039734950117232)
XLA Ops:
  0.6 0.8 %slice_bitcast_fusion = (f32[64]{0:T(128)S(1)}, f32[64]{0:T(128)S(1)}) fusion(f32[2,64]{1,0:T(2,128)} %inv_d.1), kind=kLoop, calls=%fused_computation.2 | loop fusion | bytes 1024 | tf_op jit(solution)/shard_map/mul | solution.py:412
  1.4 70.3 %shard_map.113 = (f32[64,768]{1,0:T(8,128)}, f32[64,768]{1,0:T(8,128)}, f32[64,768]{1,0:T(8,128)}, f32[64,768]{1,0:T(8,128)}) custom-call(f32[1024,768]{1,0:T(8,128)} %prior_hbm.1, f32[1,1024]{1,0:T(1,128)} %bitcast.7, f32[1,1024]{1,0:T(1,128)} %bitcast.8, s32[1,1024]{1,0:T(1,128)} %bitcast.9, s32[2,256]{1,0:T(2,128)} %pivots.1, f32[64,768]{1,0:T(8,128)} %a_one.1, ...), custom_call_target="tpu_custom_call" | custom-call | tf_op jit(solution)/shard_map/pallas_call | solution.py:374
  71.7 2.1 %multiply_add_fusion = (f32[64,768]{1,0:T(8,128)}, f32[64,768]{1,0:T(8,128)}) fusion(f32[64,768]{1,0:T(8,128)} %get-tuple-element.9, f32[64,768]{1,0:T(8,128)} %get-tuple-element.8, f32[64]{0:T(128)S(1)} %get-tuple-element.10, f32[64,768]{1,0:T(8,128)} %get-tuple-element.7, f32[64,768]{1,0:T(8,128)} %get-tuple-element.6, f32[64]{0:T(128)S(1)} %get-tuple-element.11), kind=kLoop, calls=%fused_computation | loop fusion | flops 196608 | bytes 1180160 | tf_op jit(solution)/shard_map/add | solution.py:412

commit v4 on v3

--- a/solution.py
+++ b/solution.py
@@ -135,25 +135,26 @@
         def _():
             post(q).start()
 
-    def move(buf, item, send, sem_at, rsem, to):
+    half = dense.shape[1] // 2
+
+    def piece_to(item, which, to, h):
+        at = dense.at[item, pl.ds(h * half, half)]
         return pltpu.make_async_remote_copy(
-            src_ref=buf.at[item], dst_ref=buf.at[item], send_sem=send.at[sem_at], recv_sem=rsem.at[item],
-            device_id={"wide": to, "narrow": n}, device_id_type=mesh_ids,
+            src_ref=at, dst_ref=at, send_sem=(s_right, s_left, s_pair)[which].at[item // 2, h],
+            recv_sem=recv.at[item, h], device_id={"wide": to, "narrow": n}, device_id_type=mesh_ids,
         )
 
-    def piece_to(item, which, to):
-        return move(dense, item, (s_right, s_left, s_pair)[which], item // 2, recv, to)
-
-    def send_own(make):
-        @pl.when(has_right)
-        def _():
-            make(w, 0, w + 2).start()
-
-        @pl.when(has_left)
-        def _():
-            make(w, 1, w - 2).start()
-
-        make(w, 2, pair).start()
+    def send_own():
+        for h in range(2):
+            @pl.when(has_right)
+            def _():
+                piece_to(w, 0, w + 2, h).start()
+
+            @pl.when(has_left)
+            def _():
+                piece_to(w, 1, w - 2, h).start()
+
+            piece_to(w, 2, pair, h).start()
 
     slots = n_wide * cap
     put[...] = onehot(column(owner * cap + rank) == count((2 * panel, slots), 1))
@@ -199,7 +200,7 @@
         ordered = dot(hi, put_a[...]) + dot(lo, put_a[...])
         for i in range(strips):
             dense[w, 2 * panel + i * rows_a:2 * panel + (i + 1) * rows_a, :] = ordered[:, i * kk:(i + 1) * kk]
-        send_own(piece_to)
+        send_own()
 
     def fold(v):
         return v.reshape(n_narrow, blocks, v.shape[-1])
@@ -220,25 +221,28 @@
             part[:, :, cs] += fold(dot3(ch[:panel], cl[:panel], ph, pq))
             part2[:, :, cs] += fold(dot3(ch[panel:], cl[panel:], ph, pq))
 
-    def relay_item(make, item, ahead, which, to):
-        make(item, 0, pair).wait_recv()
-        make(item, 2, pair).start()
+    def relay_item(item, ahead, which, to, h):
+        piece_to(item, 0, pair, h).wait_recv()
 
         @pl.when(ahead)
         def _():
-            make(item, which, to).start()
+            piece_to(item, which, to, h).start()
+
+        piece_to(item, 2, pair, h).start()
 
     def step(t, _):
-        @pl.when((t < line) & (a - t >= 0) & (a - t < held))
-        def _():
-            relay_item(piece_to, w - 2 * t, has_right, 0, w + 2)
-
-        @pl.when((t < line) & (a + t < held))
-        def _():
-            relay_item(piece_to, w + 2 * t, has_left, 1, w - 2)
+        for h in range(2):
+            @pl.when((t < line) & (a - t >= 0) & (a - t < held))
+            def _():
+                relay_item(w - 2 * t, has_right, 0, w + 2, h)
+
+            @pl.when((t < line) & (a + t < held))
+            def _():
+                relay_item(w + 2 * t, has_left, 1, w - 2, h)
 
         def pair_at(p):
-            piece_to(2 * p + (1 - b), 0, pair).wait_recv()
+            for h in range(2):
+                piece_to(2 * p + (1 - b), 0, pair, h).wait_recv()
             add_pair(p)
 
         @pl.when((a - t + 1 >= 0) & (a - t + 1 < held))
@@ -340,15 +344,16 @@
 
     def drain(t, _):
         item = t * 2 + b
-        piece_to(item, 2, pair).wait_send()
-
-        @pl.when((t <= a) & has_right)
-        def _():
-            piece_to(item, 0, pair).wait_send()
-
-        @pl.when((t >= a) & has_left)
-        def _():
-            piece_to(item, 1, pair).wait_send()
+        for h in range(2):
+            piece_to(item, 2, pair, h).wait_send()
+
+            @pl.when((t <= a) & has_right)
+            def _():
+                piece_to(item, 0, pair, h).wait_send()
+
+            @pl.when((t >= a) & has_left)
+            def _():
+                piece_to(item, 1, pair, h).wait_send()
 
         return 0
 
@@ -397,7 +402,7 @@
             vm((n_narrow, blocks, ext), F32),
             vm((panel, panel), F32),
             dma((pieces,)), dma((pieces,)), dma((n_wide,)),
-            dma((line,)), dma((line,)), dma((line,)), dma((pieces,)),
+            dma((line, 2)), dma((line, 2)), dma((line, 2)), dma((pieces, 2)),
             dma((chips,)), dma((chips,)), dma((chips,)), dma((chips,)),
             dma((chips,)), dma((chips,)), dma((chips,)), dma((chips,)),
             dma((chips,)), dma((n_narrow,)), dma((chips,)), dma((n_narrow,)),

time: 73.9 us -> 72.3 us (0.978)
  Pallas kernels: 70.3 us -> 68.7 us
    pallas_call x1, Pallas kernels: 70.3 us -> 68.7 us  [shards(): pl.pallas_call(functools.partial(kernel, n_wide, n_narrow, cap, pieces),...]
where the time goes in v4:
time: 72.3 us; the launch traced here: 72.1 us
  Pallas kernels  68.7 us (95%)
  other arithmetic  2.07 us (3%)
  local copies, waits for them, and re-layouts  0.76 us (1%)
    pallas_call x1, Pallas kernels, shards(): pl.pallas_call(functools.partial(kernel, n_wide, n_narrow, cap, pieces),...  68.7 us
    add x1, other arithmetic, shards(): inv_d[1][:, None] * w_two + side_two  2.07 us

profile of v4, /device:TPU:0, one launch (start us, length us, event | category | flops | bytes accessed | tf_op | source)
XLA Modules:
  0.0 72.1 jit_solution(3461042694765089541)
XLA Ops:
  0.6 0.8 %slice_bitcast_fusion = (f32[64]{0:T(128)S(1)}, f32[64]{0:T(128)S(1)}) fusion(f32[2,64]{1,0:T(2,128)} %inv_d.1), kind=kLoop, calls=%fused_computation.2 | loop fusion | bytes 1024 | tf_op jit(solution)/shard_map/mul | solution.py:417
  1.4 68.7 %shard_map.113 = (f32[64,768]{1,0:T(8,128)}, f32[64,768]{1,0:T(8,128)}, f32[64,768]{1,0:T(8,128)}, f32[64,768]{1,0:T(8,128)}) custom-call(f32[1024,768]{1,0:T(8,128)} %prior_hbm.1, f32[1,1024]{1,0:T(1,128)} %bitcast.7, f32[1,1024]{1,0:T(1,128)} %bitcast.8, s32[1,1024]{1,0:T(1,128)} %bitcast.9, s32[2,256]{1,0:T(2,128)} %pivots.1, f32[64,768]{1,0:T(8,128)} %a_one.1, ...), custom_call_target="tpu_custom_call" | custom-call | tf_op jit(solution)/shard_map/pallas_call | solution.py:379
  70.1 2.1 %multiply_add_fusion = (f32[64,768]{1,0:T(8,128)}, f32[64,768]{1,0:T(8,128)}) fusion(f32[64,768]{1,0:T(8,128)} %get-tuple-element.9, f32[64,768]{1,0:T(8,128)} %get-tuple-element.8, f32[64]{0:T(128)S(1)} %get-tuple-element.10, f32[64,768]{1,0:T(8,128)} %get-tuple-element.7, f32[64,768]{1,0:T(8,128)} %get-tuple-element.6, f32[64]{0:T(128)S(1)} %get-tuple-element.11), kind=kLoop, calls=%fused_computation | loop fusion | flops 196608 | bytes 1180160 | tf_op jit(solution)/shard_map/add | solution.py:417
